TPU v7x, 32 devices: a whole 2x2x4 slice. The times are simulated.
32 devices in a mesh: section: 4 (over z), token: 4 (over x, core), feature: 2 (over y).
Axes of the slice: x: 2, y: 2, z: 4, core: 2. Of those that a mesh axis runs over, the one named last changes fastest.
Arguments:
- residual: bfloat16 [4, 2048, 4608], P('section', 'token'), may hold values from -6 to 6
- encoder: bfloat16 [4, 4608, 8192], P('section', None, 'feature'), may hold values from -0.09375 to 0.09375
- encoder_bias: float32 [4, 8192], P('section', 'feature'), may hold values from -0.6 to 0.3
- decoder: bfloat16 [4, 4, 8192, 4608], P('section', 'token', None, 'feature'), may hold values from -0.125 to 0.125
- active: int32 [4, 32, 16], P('section'), may hold values from 0 to 3
Outputs:
- activations: bfloat16 [4, 2048, 8192], P('section', 'token', 'feature')
- reconstruction: bfloat16 [4, 2048, 4608], P('token', 'section', 'feature')
Inputs may be any that keep to these rules, and one draw needn't show every extreme that they name: Which of the 4 blocks of a group is active, for each section and tile of 64 tokens.
All inputs are finite; a program needn't handle non-finite values.
Results may differ from a plain program's by a relative error of at most 0.0049.
Values may be sent and summed in bfloat16 or wider, within the bound.
A program may use at most 256 MiB of HBM per device.

v0:
```python
import jax
import jax.numpy as jnp
from jax import lax
from jax.sharding import PartitionSpec as P

G = 16
BPG = 4
TILE = 64
BLOCK = 128


def decode_tiles(block_codes, picked, weights):
    flags = (picked[..., None] == jnp.arange(BPG, dtype=jnp.int32)).astype(jnp.bfloat16)
    dense = block_codes[:, :, :, :, None, :] * flags[:, :, None, :, :, None]
    return jnp.einsum("qptgbc,qgbcd->qptd", dense, weights, preferred_element_type=jnp.float32)


def body(residual, encoder, encoder_bias, decoder, active):
    section = lax.axis_index("section")
    token_place = lax.axis_index("token")
    feature_place = lax.axis_index("feature")
    feature_count = lax.axis_size("feature")
    rows_here = residual.shape[1]
    width_local = decoder.shape[3]
    groups_local = G // feature_count
    tile_count = rows_here // TILE
    hidden = jnp.dot(residual[0], encoder[0], preferred_element_type=jnp.float32) + encoder_bias[0]
    feature_codes = jax.nn.relu(hidden).astype(jnp.bfloat16)
    own_active = lax.dynamic_slice(
        active[0],
        (token_place * tile_count, feature_place * groups_local),
        (tile_count, groups_local),
    )
    own_flags = (own_active[..., None] == jnp.arange(BPG, dtype=jnp.int32)).astype(jnp.bfloat16)
    blocks = feature_codes.reshape(tile_count, TILE, groups_local, BPG, BLOCK)
    compact = jnp.einsum("ptgbc,pgb->ptgc", blocks, own_flags, preferred_element_type=jnp.float32)
    compact = compact.astype(jnp.bfloat16).reshape(rows_here, groups_local * BLOCK)
    dec_groups = decoder[0, 0].reshape(G, BPG, BLOCK, width_local)
    in_range = (token_place >= section).astype(jnp.float32)
    all_groups = lax.all_gather(compact, "feature", axis=1, tiled=True)
    arrived = lax.all_gather(all_groups, "token", axis=0, tiled=True)
    row_count = arrived.shape[0]
    piece_tiles = row_count // TILE
    block_codes = arrived.reshape(1, piece_tiles, TILE, G, BLOCK)
    picked = active[0][None]
    decoded = decode_tiles(block_codes, picked, dec_groups[None]).reshape(row_count, width_local)
    partial_value = decoded
    partial_value = partial_value * in_range
    rebuilt = lax.psum_scatter(partial_value, "section", scatter_dimension=0, tiled=True).astype(
        jnp.bfloat16
    )
    return (feature_codes[None], rebuilt[None])


def solution(mesh):
    placed = (
        P("section", "token", None),
        P("section", None, "feature"),
        P("section", "feature"),
        P("section", "token", None, "feature"),
        P("section", None, None),
    )
    return jax.shard_map(
        body,
        mesh=mesh,
        in_specs=placed,
        out_specs=(P("section", "token", "feature"), P("token", "section", "feature")),
        check_vma=False,
    )
```

profile of v0, /device:TPU:0, one launch (start us, length us, event | category | flops | bytes accessed | tf_op | source)
XLA Modules:
  0.0 588.4 jit_solution(12981778055123432967)
XLA Ops:
  7.2 0.0 all-gather.3.cloned.1.call-start
  7.2 0.8 constant_dynamic-slice_fusion
  8.0 0.1 copy.16
  8.1 0.1 fusion.17
  8.1 26.2 %maximum_convert_fusion = bf16[512,4096]{1,0:T(8,128)(2,1)} fusion(bf16[1,4608,4096]{2,1,0:T(8,128)(2,1)} %param.6, bf16[1,512,4608]{2,1,0:T(8,128)(2,1)} %param.5, f32[4096]{0:T(1024)} %bitcast.50), kind=kOutput, calls=%fused_computation.8 | convolution fusion | flops 19333644288 | bytes 46678016 | tf_op jit(solution)/shard_map/dot_general | solution.py:27
  34.4 7.7 %reshape.40 = bf16[8,64,8,4,128]{4,3,2,1,0:T(4,128)(2,1)} reshape(bf16[512,4096]{1,0:T(8,128)(2,1)} %maximum_convert_fusion) | data formatting | bytes 8388608 | tf_op jit(solution)/shard_map/reshape | solution.py:35
  42.1 0.0 copy-start
  42.1 4.5 fusion.14
  46.6 1.2 copy.30
  47.8 1.2 copy.31
  49.1 0.0 all-gather.3.cloned.1.call-update
  49.1 0.0 all-gather.5.cloned.1.call-start
  49.1 35.9 %all-gather.3.cloned.1.call-done = bf16[512,2048]{1,0:T(8,128)(2,1)} async-done(((bf16[512,1024]{1,0:T(8,128)(2,1)}), bf16[512,2048]{1,0:T(8,128)(2,1)}) %all-gather.3.cloned.1.call-update) | async-done | bytes 2097168 | tf_op jit(solution)/shard_map/all_gather | solution.py:40
  85.1 0.0 all-gather.5.cloned.1.call-update
  85.1 0.2 reduce-scatter.2.cloned.1.call-start
  85.3 0.0 copy-done
  85.4 0.3 mul.46
  85.7 0.5 mul.47
  86.2 58.8 %all-gather.5.cloned.1.call-done = bf16[2048,2048]{1,0:T(8,128)(2,1)} async-done(((bf16[512,2048]{1,0:T(8,128)(2,1)}), bf16[2048,2048]{1,0:T(8,128)(2,1)}) %all-gather.5.cloned.1.call-update) | async-done | bytes 8388624 | tf_op jit(solution)/shard_map/all_gather | solution.py:41
  144.9 9.8 %copy.18 = bf16[256,8,16,128]{3,2,1,0:T(8,128)(2,1)} copy(bf16[256,8,16,128]{3,1,2,0:T(8,128)(2,1)} %bitcast.43) | data formatting | bytes 16777216
  154.7 8.9 %copy.10 = bf16[2048,128,16]{1,0,2:T(8,128)(2,1)} copy(bf16[2048,128,16]{1,2,0:T(8,128)(2,1)} %bitcast.42) | data formatting | bytes 16777216 | tf_op jit(solution)/shard_map/mul | solution.py:14
  163.6 100.3 %bitcast_multiply_fusion = f32[2048,2304]{1,0:T(8,128)} fusion(bf16[16,4,128,2304]{3,2,1,0:T(8,128)(2,1)} %bitcast.49, bf16[2048,4,16]{0,2,1:T(8,128)(2,1)S(1)} %mul.47, bf16[2048,128,16]{1,0,2:T(8,128)(2,1)} %copy.10, f32[]{:T(128)S(6)} %convert_element_type.30), kind=kOutput, calls=%fused_computation.5 | convolution fusion | flops 77330907136 | bytes 65273860 | tf_op jit(solution)/shard_map/qptgbc,qgbcd->qptd/dot_general | solution.py:15
  263.8 0.0 reduce-scatter.2.cloned.1.call-update
  263.8 314.1 %reduce-scatter.2.cloned.1.call-done = f32[512,2304]{1,0:T(8,128)} async-done(((f32[2048,2304]{1,0:T(8,128)}), f32[512,2304]{1,0:T(8,128)}) %reduce-scatter.2.cloned.1.call-update) | async-done | bytes 4718608 | tf_op jit(solution)/shard_map/reduce_scatter | solution.py:49
  577.9 4.0 convert_bitcast_fusion
  (1 shorter events, 0.0 us)
Async XLA Ops:
  7.2 77.9 %all-gather.3.cloned.1.call-start = ((), (), s32[]{:S(2)}) async-start(), calls=%async_computation.1 | async-start | bytes 3145728 | tf_op jit(solution)/shard_map/all_gather | solution.py:40
  42.1 43.3 %copy-start = (s32[1,32,16]{1,2,0:T(8,128)S(1)}, s32[1,32,16]{1,2,0:T(8,128)}, u32[]{:S(2)}) copy-start(s32[1,32,16]{1,2,0:T(8,128)} %param.9) | copy-start | bytes 6148
  49.1 95.8 %all-gather.5.cloned.1.call-start = ((), (), s32[]{:S(2)}) async-start(), calls=%async_computation.2 | async-start | bytes 10485760 | tf_op jit(solution)/shard_map/all_gather | solution.py:41
  85.1 492.8 %reduce-scatter.2.cloned.1.call-start = ((), (), s32[]{:S(2)}) async-start(), calls=%async_computation.3 | async-start | bytes 23592960 | tf_op jit(solution)/shard_map/reduce_scatter | solution.py:49
Sparse Core Ops, SparseCore 0:
  49.2 35.8 all-gather.2
  86.6 58.2 all-gather.4
  264.0 313.9 reduce-scatter.1
where the time goes:
time: 589 us; the launch traced here: 588 us
  waiting for transfers between devices  409 us (69%)
  matrix products  131 us (22%)
  local copies, waits for them, and re-layouts  30.4 us (5%)
  between operations  13.8 us (2%)
    reduce_scatter x1, waiting for transfers between devices, body(): lax.psum_scatter(partial_value, 'section', scatter_dimension=0, tiled=True)  314 us
    dot_general x1, matrix products, decode_tiles(): jnp.einsum('qptgbc,qgbcd->qptd', dense, weights, preferred_element_type=j...  100 us
    all_gather x1, waiting for transfers between devices, body(): arrived = lax.all_gather(all_groups, 'token', axis=0, tiled=True)  58.8 us
    all_gather x1, waiting for transfers between devices, body(): all_groups = lax.all_gather(compact, 'feature', axis=1, tiled=True)  35.9 us
    dot_general x1, matrix products, body(): jnp.dot(residual[0], encoder[0], preferred_element_type=jnp.float32)  26.2 us
  transfers between devices with their start and end apart: 3, of which 3 were waited for; matrix products, arithmetic and copies ran while one was open for 0% of the time, Pallas kernels for 0%

commit v1 on v0

--- a/solution.py
+++ b/solution.py
@@ -38,7 +38,14 @@
     dec_groups = decoder[0, 0].reshape(G, BPG, BLOCK, width_local)
     in_range = (token_place >= section).astype(jnp.float32)
     all_groups = lax.all_gather(compact, "feature", axis=1, tiled=True)
-    arrived = lax.all_gather(all_groups, "token", axis=0, tiled=True)
+    ring = [all_groups]
+    for hop in range(3):
+        ring.append(lax.ppermute(ring[-1], "token", [(dev, (dev + 1) % 4) for dev in range(4)]))
+    arrived = jnp.roll(
+        jnp.concatenate(ring[::-1], axis=0),
+        (lax.axis_index("token") + 1) * ring[0].shape[0],
+        axis=0,
+    )
     row_count = arrived.shape[0]
     piece_tiles = row_count // TILE
     block_codes = arrived.reshape(1, piece_tiles, TILE, G, BLOCK)

time: 589 us -> 640 us (1.087)
  local copies, waits for them, and re-layouts: 30.4 us -> 64.1 us
  waiting for transfers between devices: 409 us -> 426 us
    ppermute x0 -> x3, waiting for transfers between devices: none -> 76.2 us  [body(): lax.ppermute(ring[-1], 'token', [(dev, (dev + 1) % 4) for dev in range(4)])]
    all_gather x1 -> x0, waiting for transfers between devices: 58.8 us -> none  [body(): arrived = lax.all_gather(all_groups, 'token', axis=0, tiled=True)]
    unnamed x5 -> x19, local copies, waits for them, and re-layouts: 11.1 us -> 43.3 us
  transfers between devices with their start and end apart: 3 -> 5, of which waited for: 3 -> 5; matrix products, arithmetic and copies ran while one was open for 0% -> 0% of each run, Pallas kernels for 0% -> 0%
where the time goes in v1:
time: 640 us
  waiting for transfers between devices  426 us (67%)
  matrix products  131 us (20%)
  local copies, waits for them, and re-layouts  64.1 us (10%)
  between operations  14.1 us (2%)
    reduce_scatter x1, waiting for transfers between devices, body(): lax.psum_scatter(partial_value, 'section', scatter_dimension=0, tiled=True)  314 us
    dot_general x1, matrix products, decode_tiles(): jnp.einsum('qptgbc,qgbcd->qptd', dense, weights, preferred_element_type=j...  100 us
    ppermute x3, waiting for transfers between devices, body(): lax.ppermute(ring[-1], 'token', [(dev, (dev + 1) % 4) for dev in range(4)])  76.2 us
    unnamed x19, local copies, waits for them, and re-layouts  43.3 us
    all_gather x1, waiting for transfers between devices, body(): all_groups = lax.all_gather(compact, 'feature', axis=1, tiled=True)  35.9 us
    dot_general x1, matrix products, body(): jnp.dot(residual[0], encoder[0], preferred_element_type=jnp.float32)  26.2 us
  transfers between devices with their start and end apart: 5, of which 5 were waited for; matrix products, arithmetic and copies ran while one was open for 0% of the time, Pallas kernels for 0%

profile of v1, /device:TPU:0, one launch (start us, length us, event | category | flops | bytes accessed | tf_op | source)
XLA Modules:
  0.0 639.6 jit_solution(4212900111778756848)
XLA Ops:
  7.2 0.0 all-gather.2.cloned.1.call-start
  7.2 0.8 constant_dynamic-slice_fusion
  8.0 0.1 copy.16
  8.1 0.1 fusion.17
  8.1 26.2 %maximum_convert_fusion = bf16[512,4096]{1,0:T(8,128)(2,1)} fusion(bf16[1,4608,4096]{2,1,0:T(8,128)(2,1)} %param.6, bf16[1,512,4608]{2,1,0:T(8,128)(2,1)} %param.5, f32[4096]{0:T(1024)} %bitcast.50), kind=kOutput, calls=%fused_computation.9 | convolution fusion | flops 19333644288 | bytes 46678016 | tf_op jit(solution)/shard_map/dot_general | solution.py:27
  34.4 0.0 copy-start.3
  34.4 7.7 %reshape.40 = bf16[8,64,8,4,128]{4,3,2,1,0:T(4,128)(2,1)} reshape(bf16[512,4096]{1,0:T(8,128)(2,1)} %maximum_convert_fusion) | data formatting | bytes 8388608 | tf_op jit(solution)/shard_map/reshape | solution.py:35
  42.1 4.5 fusion.14
  46.6 1.2 copy.30
  47.8 1.2 copy.31
  49.1 0.0 all-gather.2.cloned.1.call-update
  49.1 0.0 reduce-scatter.2.cloned.1.call-start
  49.2 35.9 %all-gather.2.cloned.1.call-done = bf16[512,2048]{1,0:T(8,128)(2,1)} async-done(((bf16[512,1024]{1,0:T(8,128)(2,1)}), bf16[512,2048]{1,0:T(8,128)(2,1)}) %all-gather.2.cloned.1.call-update) | async-done | bytes 2097168 | tf_op jit(solution)/shard_map/all_gather | solution.py:40
  85.1 0.0 copy-start
  85.1 0.0 collective-permute-start
  85.1 25.7 %collective-permute-done = bf16[512,2048]{1,0:T(8,128)(2,1)S(1)} collective-permute-done((bf16[512,2048]{1,0:T(8,128)(2,1)}, bf16[512,2048]{1,0:T(8,128)(2,1)S(1)}, u32[]{:S(2)}, u32[]{:S(2)}) %collective-permute-start) | collective-permute-done | bytes 2097184 | tf_op jit(solution)/shard_map/ppermute | solution.py:43
  110.8 0.0 copy-start.1
  110.8 1.3 copy-done.1
  112.1 0.0 collective-permute-start.1
  112.1 25.6 %collective-permute-done.1 = bf16[512,2048]{1,0:T(8,128)(2,1)} collective-permute-done((bf16[512,2048]{1,0:T(8,128)(2,1)S(1)}, bf16[512,2048]{1,0:T(8,128)(2,1)}, u32[]{:S(2)}, u32[]{:S(2)}) %collective-permute-start.1) | collective-permute-done | bytes 2097184 | tf_op jit(solution)/shard_map/ppermute | solution.py:43
  137.6 0.0 collective-permute-start.2
  137.6 0.0 copy-done.3
  137.7 0.3 mul.50
  138.0 0.5 mul.51
  138.5 0.0 copy-start.2
  138.5 24.9 %collective-permute-done.2 = bf16[512,2048]{1,0:T(8,128)(2,1)} collective-permute-done((bf16[512,2048]{1,0:T(8,128)(2,1)}, bf16[512,2048]{1,0:T(8,128)(2,1)}, u32[]{:S(2)}, u32[]{:S(2)}) %collective-permute-start.2) | collective-permute-done | bytes 2097184 | tf_op jit(solution)/shard_map/ppermute | solution.py:43
  163.4 3.2 constant_dynamic-update-slice_fusion.7
  166.6 3.2 constant_dynamic-update-slice_fusion.6
  169.8 3.2 constant_dynamic-update-slice_fusion.5
  172.9 3.2 constant_dynamic-update-slice_fusion.4
  176.1 3.2 constant_dynamic-update-slice_fusion.3
  179.3 3.2 constant_dynamic-update-slice_fusion.2
  182.5 0.0 copy-done.2
  182.5 1.5 constant_dynamic-update-slice_fusion.1
  183.9 0.0 copy-done
  183.9 1.4 constant_dynamic-update-slice_fusion
  185.4 10.3 %dynamic-slice_bitcast_fusion = bf16[256,8,16,128]{3,1,2,0:T(8,128)(2,1)} fusion(bf16[4096,2048]{1,0:T(8,128)(2,1)} %constant_dynamic-update-slice_fusion, s32[]{:T(128)S(6)} %select_n.22), kind=kLoop, calls=%fused_computation.8 | loop fusion | bytes 16777220
  195.7 9.8 %copy.18 = bf16[256,8,16,128]{3,2,1,0:T(8,128)(2,1)} copy(bf16[256,8,16,128]{3,1,2,0:T(8,128)(2,1)} %dynamic-slice_bitcast_fusion) | data formatting | bytes 16777216
  205.5 8.9 %copy.10 = bf16[2048,128,16]{1,0,2:T(8,128)(2,1)} copy(bf16[2048,128,16]{1,2,0:T(8,128)(2,1)} %bitcast.43) | data formatting | bytes 16777216 | tf_op jit(solution)/shard_map/mul | solution.py:14
  214.4 100.3 %bitcast_multiply_fusion = f32[2048,2304]{1,0:T(8,128)} fusion(bf16[16,4,128,2304]{3,2,1,0:T(8,128)(2,1)} %bitcast.49, bf16[2048,4,16]{0,2,1:T(8,128)(2,1)S(1)} %mul.51, bf16[2048,128,16]{1,0,2:T(8,128)(2,1)} %copy.10, f32[]{:T(128)S(6)} %convert_element_type.30), kind=kOutput, calls=%fused_computation.5 | convolution fusion | flops 77330907136 | bytes 65273860 | tf_op jit(solution)/shard_map/qptgbc,qgbcd->qptd/dot_general | solution.py:15
  314.6 0.0 reduce-scatter.2.cloned.1.call-update
  314.6 314.1 %reduce-scatter.2.cloned.1.call-done = f32[512,2304]{1,0:T(8,128)} async-done(((f32[2048,2304]{1,0:T(8,128)}), f32[512,2304]{1,0:T(8,128)}) %reduce-scatter.2.cloned.1.call-update) | async-done | bytes 4718608 | tf_op jit(solution)/shard_map/reduce_scatter | solution.py:56
  628.7 4.0 convert_bitcast_fusion
  (1 shorter events, 0.0 us)
Async XLA Ops:
  7.2 77.9 %all-gather.2.cloned.1.call-start = ((), (), s32[]{:S(2)}) async-start(), calls=%async_computation.1 | async-start | bytes 3145728 | tf_op jit(solution)/shard_map/all_gather | solution.py:40
  34.4 103.3 %copy-start.3 = (s32[1,32,16]{1,2,0:T(8,128)S(1)}, s32[1,32,16]{1,2,0:T(8,128)}, u32[]{:S(2)}) copy-start(s32[1,32,16]{1,2,0:T(8,128)} %param.9) | copy-start | bytes 6148
  49.1 579.6 %reduce-scatter.2.cloned.1.call-start = ((), (), s32[]{:S(2)}) async-start(), calls=%async_computation.2 | async-start | bytes 23592960 | tf_op jit(solution)/shard_map/reduce_scatter | solution.py:56
  85.1 98.9 %copy-start = (bf16[512,2048]{1,0:T(8,128)(2,1)S(1)}, bf16[512,2048]{1,0:T(8,128)(2,1)}, u32[]{:S(2)}) copy-start(bf16[512,2048]{1,0:T(8,128)(2,1)} %all-gather.2.cloned.1.call-done) | copy-start | bytes 6291460
  85.1 25.7 %collective-permute-start = (bf16[512,2048]{1,0:T(8,128)(2,1)}, bf16[512,2048]{1,0:T(8,128)(2,1)S(1)}, u32[]{:S(2)}, u32[]{:S(2)}) collective-permute-start(bf16[512,2048]{1,0:T(8,128)(2,1)} %all-gather.2.cloned.1.call-done), channel_id=1, source_target_pairs={{0,2},{2,4},{4,6},{6,0},{1,3},{3,5},{5,7},{7,1},{8,10},{10,12},{12... | collective-permute-start | bytes 6291464 | tf_op jit(solution)/shard_map/ppermute | solution.py:43
  110.8 1.3 copy-start.1
  112.1 25.6 %collective-permute-start.1 = (bf16[512,2048]{1,0:T(8,128)(2,1)S(1)}, bf16[512,2048]{1,0:T(8,128)(2,1)}, u32[]{:S(2)}, u32[]{:S(2)}) collective-permute-start(bf16[512,2048]{1,0:T(8,128)(2,1)S(1)} %collective-permute-done), channel_id=1, source_target_pairs={{0,2},{2,4},{4,6},{6,0},{1,3},{3,5},{5,7},{7,1},{8,10},{10,12},{12... | collective-permute-start | bytes 6291464 | tf_op jit(solution)/shard_map/ppermute | solution.py:43
  137.6 25.8 %collective-permute-start.2 = (bf16[512,2048]{1,0:T(8,128)(2,1)}, bf16[512,2048]{1,0:T(8,128)(2,1)}, u32[]{:S(2)}, u32[]{:S(2)}) collective-permute-start(bf16[512,2048]{1,0:T(8,128)(2,1)} %collective-permute-done.1), channel_id=1, source_target_pairs={{0,2},{2,4},{4,6},{6,0},{1,3},{3,5},{5,7},{7,1},{8,10},{10,12},{12... | collective-permute-start | bytes 6291464 | tf_op jit(solution)/shard_map/ppermute | solution.py:43
  138.5 44.0 %copy-start.2 = (bf16[512,2048]{1,0:T(8,128)(2,1)S(1)}, bf16[512,2048]{1,0:T(8,128)(2,1)}, u32[]{:S(2)}) copy-start(bf16[512,2048]{1,0:T(8,128)(2,1)} %copy-done.1) | copy-start | bytes 6291460
Sparse Core Ops, SparseCore 0:
  49.2 35.8 all-gather.1
  314.8 313.9 reduce-scatter.1
